TPU v7x, 128 devices: a whole 4x4x4 slice. The times are simulated.
128 devices in a mesh: rep: 16 (over x, z), grp: 8 (over y, core).
Axes of the slice: x: 4, y: 4, z: 4, core: 2. Of those that a mesh axis runs over, the one named last changes fastest.
Arguments:
- inputs: bfloat16 [2, 262144, 1152], P(None, ('rep', 'grp')), may hold values from -6 to 6
- out_grads: bfloat16 [2, 262144, 1152], P(None, ('rep', 'grp')), may hold values from -6 to 6
- weights: bfloat16 [2, 1152, 1152], P(None, 'grp'), may hold values from -3 to 3
- biases: bfloat16 [2, 1152], P(None, 'grp'), may hold values from -3 to 3
- errors: float32 [16, 2, 1152, 1152], P('rep', None, 'grp'), may hold values from -6 to 6
- momenta: float32 [2, 1152, 1152], P(None, 'grp'), may hold values from -3 to 3
- bias_momenta: float32 [2, 1152], P(None, 'grp'), may hold values from -3 to 3
- q_start: float32 [2, 1152, 32], replicated, may hold values from -6 to 6
Outputs:
- new_weights: bfloat16 [2, 1152, 1152], replicated
- new_biases: bfloat16 [2, 1152], replicated
- new_errors: float32 [16, 2, 1152, 1152], P('rep', None, 'grp')
- new_momenta: float32 [2, 1152, 1152], P(None, 'grp')
- new_bias_momenta: float32 [2, 1152], P(None, 'grp')
All inputs are finite; a program needn't handle non-finite values.
Results may differ from a plain program's by a relative error of at most 0.0045.
Values may be sent and summed in bfloat16 or wider, within the bound.
No kernel may reach another device: no remote copies, remote signals or barrier semaphores. Data moves between devices by JAX's collectives and lax.ppermute only.
A program may use at most 256 MiB of HBM per device.

v0:
```python
import jax
import jax.numpy as jnp
from jax import lax
from jax.sharding import PartitionSpec as P

ROUNDS = 2
NS_STEPS = 5
HIGH = lax.Precision.HIGHEST


def orthonormal(p_sum, gram):
    fro = jnp.sqrt(jnp.sum(gram * gram, axis=(1, 2))) + 1e-06
    scaled = gram / fro[:, None, None]
    eye = jnp.eye(gram.shape[-1], dtype=jnp.float32)
    ymat = scaled
    zmat = jnp.broadcast_to(eye, gram.shape)
    for step in range(NS_STEPS):
        tmat = 1.5 * eye - 0.5 * jnp.einsum("lab,lbc->lac", zmat, ymat, precision=HIGH)
        ymat = jnp.einsum("lab,lbc->lac", ymat, tmat, precision=HIGH)
        zmat = jnp.einsum("lab,lbc->lac", tmat, zmat, precision=HIGH)
    phat = jnp.einsum("lrk,lkj->lrj", p_sum, zmat, precision=HIGH)
    return phat / jnp.sqrt(fro)[:, None, None]


def body(inputs, out_grads, weights, biases, errors, momenta, bias_momenta, q_start):
    layers = inputs.shape[0]
    tok = inputs.shape[1]
    width = inputs.shape[2]
    groups = lax.axis_size("grp")
    reps = lax.axis_size("rep")
    rows = width // groups
    scale = float(tok) ** (-0.5)
    grads = []
    for layer in range(layers):
        x_layer = inputs[layer]
        y_layer = out_grads[layer]

        def term(start, count, x_layer=x_layer, y_layer=y_layer):
            return jnp.einsum("tr,te->re", x_layer, y_layer, preferred_element_type=jnp.float32)

        grads.append(
            lax.psum_scatter(
                term(jnp.int32(0), lax.axis_size("grp") * rows),
                "grp",
                scatter_dimension=0,
                tiled=True,
            )
        )
    merged = jnp.stack(grads) * scale + errors[0]
    col_sums = jnp.sum(out_grads, axis=1, dtype=jnp.float32)
    bias_total = lax.psum(col_sums, ("rep", "grp")) * (scale / reps)
    bias_rows = biases.shape[1]
    bias_grad = lax.dynamic_slice_in_dim(
        bias_total, lax.axis_index("grp") * bias_rows, bias_rows, 1
    )
    qmat = q_start
    phat = None
    for rnd in range(ROUNDS):
        local_p = jnp.einsum("lre,lek->lrk", merged, qmat, precision=HIGH)
        p_sum = lax.psum(local_p, "rep")
        local_gram = jnp.einsum("lrk,lrj->lkj", p_sum, p_sum, precision=HIGH)
        gram = lax.psum(local_gram, "grp")
        phat = orthonormal(p_sum, gram)
        local_q = jnp.einsum("lre,lrk->lek", merged, phat, precision=HIGH)
        qmat = lax.psum(local_q, ("rep", "grp"))
    approx = jnp.einsum("lrk,lek->lre", phat, qmat, precision=HIGH) / reps
    new_errors = (merged - approx)[None]
    new_momenta = 0.9 * momenta + approx
    weight_shard = (weights.astype(jnp.float32) - 0.5 * new_momenta).astype(jnp.bfloat16)
    new_bias_momenta = 0.9 * bias_momenta + bias_grad
    bias_shard = (biases.astype(jnp.float32) - 0.5 * new_bias_momenta).astype(jnp.bfloat16)
    new_weights, new_biases = (
        lax.all_gather(weight_shard, "grp", axis=1, tiled=True),
        lax.all_gather(bias_shard, "grp", axis=1, tiled=True),
    )
    return (new_weights, new_biases, new_errors, new_momenta, new_bias_momenta)


def solution(mesh):
    placed = (
        P(None, ("rep", "grp"), None),
        P(None, ("rep", "grp"), None),
        P(None, "grp", None),
        P(None, "grp"),
        P("rep", None, "grp", None),
        P(None, "grp", None),
        P(None, "grp"),
        P(),
    )
    return jax.shard_map(
        body,
        mesh=mesh,
        in_specs=placed,
        out_specs=(P(), P(), P("rep", None, "grp", None), P(None, "grp", None), P(None, "grp")),
        check_vma=False,
    )
```

profile of v0, /device:TPU:1, one launch (start us, length us, event | category | flops | bytes accessed | tf_op | source)
XLA Modules:
  0.0 687.0 jit_solution(1677941259270240270)
XLA Ops:
  7.2 12.5 %fusion.3 = f32[1152,1152]{1,0:T(8,128)} fusion(bf16[2,2048,1152]{2,1,0:T(8,128)(2,1)} %param.9, bf16[2,2048,1152]{2,1,0:T(8,128)(2,1)} %param.8), kind=kOutput, calls=%fused_computation.4 | convolution fusion | flops 5435817984 | bytes 14745600 | tf_op jit(solution)/shard_map/tr,te->re/dot_general | solution.py:39
  19.9 12.5 %fusion = f32[1152,1152]{1,0:T(8,128)} fusion(bf16[2,2048,1152]{2,1,0:T(8,128)(2,1)} %param.9, bf16[2,2048,1152]{2,1,0:T(8,128)(2,1)} %param.8), kind=kOutput, calls=%fused_computation.1 | convolution fusion | flops 5435817984 | bytes 14745600 | tf_op jit(solution)/shard_map/tr,te->re/dot_general | solution.py:39
  32.6 28.2 %reduce-scatter.3.cloned.1.call-done = f32[144,1152]{1,0:T(8,128)} async-done(((f32[1152,1152]{1,0:T(8,128)}), f32[144,1152]{1,0:T(8,128)}) %reduce-scatter.3.cloned.1.call-update) | async-done | bytes 663568 | tf_op jit(solution)/shard_map/reduce_scatter | solution.py:42
  60.7 42.6 %reduce-scatter.5.cloned.1.call-done = f32[144,1152]{1,0:T(8,128)} async-done(((f32[1152,1152]{1,0:T(8,128)}), f32[144,1152]{1,0:T(8,128)}) %reduce-scatter.5.cloned.1.call-update) | async-done | bytes 663568 | tf_op jit(solution)/shard_map/reduce_scatter | solution.py:42
  103.3 1.4 fusion.10
  104.8 1.5 fusion.36
  106.3 60.4 %psum.49 = f32[2,144,32]{1,2,0:T(8,128)S(1)} all-reduce(f32[2,144,32]{1,2,0:T(8,128)S(1)} %fusion.36), channel_id=1, replica_groups=mesh['rep'=16,'grp'=8] {'rep'}, use_global_device_ids=true, to_apply=%region_2.0 | all-reduce | flops 9216 | bytes 73728 | tf_op jit(solution)/shard_map/psum | solution.py:60
  166.9 37.5 %psum.50 = f32[2,32,32]{2,1,0:T(8,128)S(1)} all-reduce(f32[2,32,32]{2,1,0:T(8,128)S(1)} %fusion.37), channel_id=1, replica_groups=mesh['rep'=16,'grp'=8] {'grp'}, use_global_device_ids=true, to_apply=%region_3.0 | all-reduce | flops 2048 | bytes 16384 | tf_op jit(solution)/shard_map/psum | solution.py:62
  204.4 0.2 fusion.20
  207.2 1.6 fusion.45
  208.9 139.4 %all-reduce.3.cloned.1.call-done = f32[2,1152,32]{1,2,0:T(8,128)} async-done(((f32[2,1152,32]{1,2,0:T(8,128)}), f32[2,1152,32]{1,2,0:T(8,128)}) %all-reduce.3.cloned.1.call-update) | async-done | bytes 294928 | tf_op jit(solution)/shard_map/psum | solution.py:65
  348.4 2.5 fusion.46
  350.9 58.2 %psum.52 = f32[2,144,32]{1,2,0:T(8,128)S(1)} all-reduce(f32[2,144,32]{1,2,0:T(8,128)S(1)} %fusion.46), channel_id=1, replica_groups=mesh['rep'=16,'grp'=8] {'rep'}, use_global_device_ids=true, to_apply=%region_6.0 | all-reduce | flops 9216 | bytes 73728 | tf_op jit(solution)/shard_map/psum | solution.py:60
  409.3 35.9 %psum.53 = f32[2,32,32]{2,1,0:T(8,128)S(1)} all-reduce(f32[2,32,32]{2,1,0:T(8,128)S(1)} %fusion.47), channel_id=1, replica_groups=mesh['rep'=16,'grp'=8] {'grp'}, use_global_device_ids=true, to_apply=%region_7.0 | all-reduce | flops 2048 | bytes 16384 | tf_op jit(solution)/shard_map/psum | solution.py:62
  445.3 0.2 fusion.15
  448.2 1.6 fusion.55
  449.8 139.4 %all-reduce.5.cloned.1.call-done = f32[2,1152,32]{1,2,0:T(8,128)} async-done(((f32[2,1152,32]{1,2,0:T(8,128)}), f32[2,1152,32]{1,2,0:T(8,128)}) %all-reduce.5.cloned.1.call-update) | async-done | bytes 294928 | tf_op jit(solution)/shard_map/psum | solution.py:65
  589.2 4.4 subtract_convert_fusion
  593.7 5.0 convert_reduce_fusion
  598.7 65.3 %psum.55 = f32[2,1152]{1,0:T(2,128)S(1)} all-reduce(f32[2,1152]{1,0:T(2,128)S(1)} %convert_reduce_fusion), channel_id=1, replica_groups=mesh['rep'=16,'grp'=8] {'rep','grp'}, use_global_device_ids=true, to_apply=%region_11.0 | all-reduce | flops 2304 | bytes 18432 | tf_op jit(solution)/shard_map/psum | solution.py:51
  664.0 0.7 fusion.32
  664.6 9.9 %all-gather = bf16[8,144,2]{1,2,0:T(2,128)(2,1)S(1)} all-gather(bf16[1,144,2]{1,2,0:T(2,128)(2,1)S(1)} %get-tuple-element.5), channel_id=1, replica_groups=mesh['rep'=16,'grp'=8] {'grp'}, dimensions={0}, use_global_device_ids=true | all-gather | bytes 5184 | tf_op jit(solution)/shard_map/all_gather | solution.py:74
  674.5 0.7 reshape.33
  675.2 5.3 copy.22
  (58 shorter events, 6.0 us)
Async XLA Ops:
  7.2 97.6 %copy-start = (f32[2,1152,32]{1,2,0:T(8,128)S(1)}, f32[2,1152,32]{1,2,0:T(8,128)}, u32[]{:S(2)}) copy-start(f32[2,1152,32]{1,2,0:T(8,128)} %param.15) | copy-start | bytes 884740
  7.2 53.5 %reduce-scatter.3.cloned.1.call-start = ((), (), s32[]{:S(2)}) async-start(), calls=%async_computation.2 | async-start | bytes 5971968 | tf_op jit(solution)/shard_map/reduce_scatter | solution.py:42
  19.7 83.6 %reduce-scatter.5.cloned.1.call-start = ((), (), s32[]{:S(2)}) async-start(), calls=%async_computation.3 | async-start | bytes 5971968 | tf_op jit(solution)/shard_map/reduce_scatter | solution.py:42
  32.5 70.8 %copy-start.1 = (f32[1,2,144,1152]{3,2,1,0:T(8,128)S(1)}, f32[1,2,144,1152]{3,2,1,0:T(8,128)}, u32[]{:S(2)}) copy-start(f32[1,2,144,1152]{3,2,1,0:T(8,128)} %param.12) | copy-start | bytes 3981316
  32.5 315.9 %all-reduce.3.cloned.1.call-start = ((), (), s32[]{:S(2)}) async-start(), calls=%async_computation.4 | async-start | bytes 589824 | tf_op jit(solution)/shard_map/psum | solution.py:65
  208.9 380.4 %all-reduce.5.cloned.1.call-start = ((), (), s32[]{:S(2)}) async-start(), calls=%async_computation.5 | async-start | bytes 589824 | tf_op jit(solution)/shard_map/psum | solution.py:65
  447.2 142.1 %copy-start.2 = (f32[2,144,1152]{2,1,0:T(8,128)S(1)}, f32[2,144,1152]{2,1,0:T(8,128)}, u32[]{:S(2)}) copy-start(f32[2,144,1152]{2,1,0:T(8,128)} %param.13) | copy-start | bytes 3981316
  449.8 225.4 %all-gather.3.cloned.1.call-start = ((), (), s32[]{:S(2)}) async-start(), calls=%async_computation.6 | async-start | bytes 5971968 | tf_op jit(solution)/shard_map/all_gather | solution.py:73
  593.7 70.3 %copy-start.3 = (f32[2,144]{1,0:T(2,128)S(1)}, f32[2,144]{1,0:T(2,128)}, u32[]{:S(2)}) copy-start(f32[2,144]{1,0:T(2,128)} %param.14) | copy-start | bytes 3460
  593.7 70.2 %copy-start.4 = (bf16[2,144]{1,0:T(2,128)(2,1)S(1)}, bf16[2,144]{1,0:T(2,128)(2,1)}, u32[]{:S(2)}) copy-start(bf16[2,144]{1,0:T(2,128)(2,1)} %param.11) | copy-start | bytes 1732
Sparse Core Ops, SparseCore 0:
  19.8 40.8 reduce-scatter.2
  63.7 39.5 reduce-scatter.4
  209.0 139.3 all-reduce.2
  449.9 139.3 all-reduce.4
  593.8 36.2 all-gather.2
where the time goes:
time: 687 us
  waiting for transfers between devices  350 us (51%)
  blocking collectives  267 us (39%)
  matrix products  42.4 us (6%)
  between operations  14.1 us (2%)
  other arithmetic  7.32 us (1%)
    psum x2, waiting for transfers between devices, body(): qmat = lax.psum(local_q, ('rep', 'grp'))  279 us
    psum x2, blocking collectives, body(): p_sum = lax.psum(local_p, 'rep')  119 us
    psum x2, blocking collectives, body(): gram = lax.psum(local_gram, 'grp')  73.4 us
    reduce_scatter x2, waiting for transfers between devices, body(): lax.psum_scatter(term(jnp.int32(0), lax.axis_size('grp') * rows), 'grp',...  70.7 us
    psum x1, blocking collectives, body(): bias_total = lax.psum(col_sums, ('rep', 'grp')) * (scale / reps)  65.3 us
    dot_general x2, matrix products, term(): jnp.einsum('tr,te->re', x_layer, y_layer, preferred_element_type=jnp.floa...  25 us
  transfers between devices with their start and end apart: 5, of which 4 were waited for; matrix products, arithmetic and copies ran while one was open for 3% of the time, Pallas kernels for 0%

commit v1 on v0

--- a/solution.py
+++ b/solution.py
@@ -57,7 +57,9 @@
     phat = None
     for rnd in range(ROUNDS):
         local_p = jnp.einsum("lre,lek->lrk", merged, qmat, precision=HIGH)
-        p_sum = lax.psum(local_p, "rep")
+        p_sum = local_p
+        for hop in (1, 2, 4, 8):
+            p_sum = p_sum + lax.ppermute(p_sum, "rep", [(dev, dev ^ hop) for dev in range(16)])
         local_gram = jnp.einsum("lrk,lrj->lkj", p_sum, p_sum, precision=HIGH)
         gram = lax.psum(local_gram, "grp")
         phat = orthonormal(p_sum, gram)

time: 687 us -> 591 us (0.86)
  blocking collectives: 267 us -> 130 us
  waiting for transfers between devices: 350 us -> 375 us
  starting transfers between devices: 0.39 us -> 15.3 us
    psum x2 -> x0, blocking collectives: 119 us -> none  [body(): p_sum = lax.psum(local_p, 'rep')]
    psum x2, blocking collectives: 73.4 us -> 54.6 us  [body(): gram = lax.psum(local_gram, 'grp')]
    ppermute x0 -> x8, waiting for transfers between devices: none -> 16.8 us  [body(): lax.ppermute(p_sum, 'rep', [(dev, dev ^ hop) for dev in range(16)])]
    ppermute x0 -> x8, starting transfers between devices: none -> 14.7 us  [body(): lax.ppermute(p_sum, 'rep', [(dev, dev ^ hop) for dev in range(16)])]
    psum x2, waiting for transfers between devices: 279 us -> 288 us  [body(): qmat = lax.psum(local_q, ('rep', 'grp'))]
  transfers between devices with their start and end apart: 5 -> 13, of which waited for: 4 -> 12; matrix products, arithmetic and copies ran while one was open for 3% -> 3% of each run, Pallas kernels for 0% -> 0%
where the time goes in v1:
time: 591 us; the launch traced here: 590 us
  waiting for transfers between devices  375 us (63%)
  blocking collectives  130 us (22%)
  matrix products  42.4 us (7%)
  starting transfers between devices  15.3 us (3%)
  between operations  14.1 us (2%)
  other arithmetic  7.39 us (1%)
  local copies, waits for them, and re-layouts  6.02 us (1%)
    psum x2, waiting for transfers between devices, body(): qmat = lax.psum(local_q, ('rep', 'grp'))  288 us
    reduce_scatter x2, waiting for transfers between devices, body(): lax.psum_scatter(term(jnp.int32(0), lax.axis_size('grp') * rows), 'grp',...  70.8 us
    psum x1, blocking collectives, body(): bias_total = lax.psum(col_sums, ('rep', 'grp')) * (scale / reps)  65.2 us
    psum x2, blocking collectives, body(): gram = lax.psum(local_gram, 'grp')  54.6 us
    dot_general x2, matrix products, term(): jnp.einsum('tr,te->re', x_layer, y_layer, preferred_element_type=jnp.floa...  25 us
    ppermute x8, waiting for transfers between devices, body(): lax.ppermute(p_sum, 'rep', [(dev, dev ^ hop) for dev in range(16)])  16.8 us
    ppermute x8, starting transfers between devices, body(): lax.ppermute(p_sum, 'rep', [(dev, dev ^ hop) for dev in range(16)])  14.7 us
  transfers between devices with their start and end apart: 13, of which 12 were waited for; matrix products, arithmetic and copies ran while one was open for 3% of the time, Pallas kernels for 0%

profile of v1, /device:TPU:1, one launch (start us, length us, event | category | flops | bytes accessed | tf_op | source)
XLA Modules:
  0.0 590.3 jit_solution(1055742230637638989)
XLA Ops:
  7.2 12.5 %fusion.3 = f32[1152,1152]{1,0:T(8,128)} fusion(bf16[2,2048,1152]{2,1,0:T(8,128)(2,1)} %param.9, bf16[2,2048,1152]{2,1,0:T(8,128)(2,1)} %param.8), kind=kOutput, calls=%fused_computation.4 | convolution fusion | flops 5435817984 | bytes 14745600 | tf_op jit(solution)/shard_map/tr,te->re/dot_general | solution.py:39
  20.0 12.5 %fusion = f32[1152,1152]{1,0:T(8,128)} fusion(bf16[2,2048,1152]{2,1,0:T(8,128)(2,1)} %param.9, bf16[2,2048,1152]{2,1,0:T(8,128)(2,1)} %param.8), kind=kOutput, calls=%fused_computation.1 | convolution fusion | flops 5435817984 | bytes 14745600 | tf_op jit(solution)/shard_map/tr,te->re/dot_general | solution.py:39
  32.5 28.2 %reduce-scatter.3.cloned.1.call-done = f32[144,1152]{1,0:T(8,128)} async-done(((f32[1152,1152]{1,0:T(8,128)}), f32[144,1152]{1,0:T(8,128)}) %reduce-scatter.3.cloned.1.call-update) | async-done | bytes 663568 | tf_op jit(solution)/shard_map/reduce_scatter | solution.py:42
  60.7 42.6 %reduce-scatter.5.cloned.1.call-done = f32[144,1152]{1,0:T(8,128)} async-done(((f32[1152,1152]{1,0:T(8,128)}), f32[144,1152]{1,0:T(8,128)}) %reduce-scatter.5.cloned.1.call-update) | async-done | bytes 663568 | tf_op jit(solution)/shard_map/reduce_scatter | solution.py:42
  109.5 2.9 collective-permute-start.1
  115.5 1.9 collective-permute-done.2
  117.4 2.7 collective-permute-start.3
  120.2 1.9 collective-permute-done.3
  122.3 28.2 %psum.35 = f32[2,32,32]{2,1,0:T(8,128)S(1)} all-reduce(f32[2,32,32]{2,1,0:T(8,128)S(1)} %fusion.37), channel_id=1, replica_groups=mesh['rep'=16,'grp'=8] {'grp'}, use_global_device_ids=true, to_apply=%region_2.0 | all-reduce | flops 2048 | bytes 16384 | tf_op jit(solution)/shard_map/psum | solution.py:64
  155.3 145.1 %all-reduce.3.cloned.1.call-done = f32[2,1152,32]{1,2,0:T(8,128)} async-done(((f32[2,1152,32]{1,2,0:T(8,128)}), f32[2,1152,32]{1,2,0:T(8,128)}) %all-reduce.3.cloned.1.call-update) | async-done | bytes 294928 | tf_op jit(solution)/shard_map/psum | solution.py:67
  300.4 2.5 fusion.46
  304.1 2.0 collective-permute-done.4
  306.1 2.3 collective-permute-start.5
  308.4 2.4 collective-permute-done.5
  311.6 2.5 collective-permute-done.6
  314.1 2.3 collective-permute-start.7
  316.3 2.4 collective-permute-done.7
  319.0 26.4 %psum.37 = f32[2,32,32]{2,1,0:T(8,128)S(1)} all-reduce(f32[2,32,32]{2,1,0:T(8,128)S(1)} %fusion.47), channel_id=1, replica_groups=mesh['rep'=16,'grp'=8] {'grp'}, use_global_device_ids=true, to_apply=%region_5.0 | all-reduce | flops 2048 | bytes 16384 | tf_op jit(solution)/shard_map/psum | solution.py:64
  350.0 142.6 %all-reduce.5.cloned.1.call-done = f32[2,1152,32]{1,2,0:T(8,128)} async-done(((f32[2,1152,32]{1,2,0:T(8,128)}), f32[2,1152,32]{1,2,0:T(8,128)}) %all-reduce.5.cloned.1.call-update) | async-done | bytes 294928 | tf_op jit(solution)/shard_map/psum | solution.py:67
  492.6 4.4 subtract_convert_fusion
  497.0 5.0 convert_reduce_fusion
  502.0 65.2 %psum.39 = f32[2,1152]{1,0:T(2,128)S(1)} all-reduce(f32[2,1152]{1,0:T(2,128)S(1)} %convert_reduce_fusion), channel_id=1, replica_groups=mesh['rep'=16,'grp'=8] {'rep','grp'}, use_global_device_ids=true, to_apply=%region_9.0 | all-reduce | flops 2304 | bytes 18432 | tf_op jit(solution)/shard_map/psum | solution.py:51
  567.9 9.9 %all-gather = bf16[8,144,2]{1,2,0:T(2,128)(2,1)S(1)} all-gather(bf16[1,144,2]{1,2,0:T(2,128)(2,1)S(1)} %get-tuple-element.5), channel_id=1, replica_groups=mesh['rep'=16,'grp'=8] {'grp'}, dimensions={0}, use_global_device_ids=true | all-gather | bytes 5184 | tf_op jit(solution)/shard_map/all_gather | solution.py:76
  578.5 5.3 copy.22
  (80 shorter events, 22.4 us)
Async XLA Ops:
  7.2 97.6 %copy-start = (f32[2,1152,32]{1,2,0:T(8,128)S(1)}, f32[2,1152,32]{1,2,0:T(8,128)}, u32[]{:S(2)}) copy-start(f32[2,1152,32]{1,2,0:T(8,128)} %param.15) | copy-start | bytes 884740
  7.2 53.6 %reduce-scatter.3.cloned.1.call-start = ((), (), s32[]{:S(2)}) async-start(), calls=%async_computation.2 | async-start | bytes 5971968 | tf_op jit(solution)/shard_map/reduce_scatter | solution.py:42
  19.7 83.6 %reduce-scatter.5.cloned.1.call-start = ((), (), s32[]{:S(2)}) async-start(), calls=%async_computation.3 | async-start | bytes 5971968 | tf_op jit(solution)/shard_map/reduce_scatter | solution.py:42
  32.5 70.8 %copy-start.1 = (f32[1,2,144,1152]{3,2,1,0:T(8,128)S(1)}, f32[1,2,144,1152]{3,2,1,0:T(8,128)}, u32[]{:S(2)}) copy-start(f32[1,2,144,1152]{3,2,1,0:T(8,128)} %param.12) | copy-start | bytes 3981316
  32.5 267.9 %all-reduce.3.cloned.1.call-start = ((), (), s32[]{:S(2)}) async-start(), calls=%async_computation.4 | async-start | bytes 589824 | tf_op jit(solution)/shard_map/psum | solution.py:67
  106.3 3.2 collective-permute-start
  109.5 4.7 collective-permute-start.1
  114.2 3.2 collective-permute-start.2
  117.4 4.7 collective-permute-start.3
  155.0 337.5 %all-reduce.5.cloned.1.call-start = ((), (), s32[]{:S(2)}) async-start(), calls=%async_computation.5 | async-start | bytes 589824 | tf_op jit(solution)/shard_map/psum | solution.py:67
  302.9 3.2 collective-permute-start.4
  306.1 4.7 collective-permute-start.5
  310.8 3.2 collective-permute-start.6
  314.1 4.7 collective-permute-start.7
  347.4 145.2 %copy-start.2 = (f32[2,144,1152]{2,1,0:T(8,128)S(1)}, f32[2,144,1152]{2,1,0:T(8,128)}, u32[]{:S(2)}) copy-start(f32[2,144,1152]{2,1,0:T(8,128)} %param.13) | copy-start | bytes 3981316
  349.9 228.6 %all-gather.3.cloned.1.call-start = ((), (), s32[]{:S(2)}) async-start(), calls=%async_computation.6 | async-start | bytes 5971968 | tf_op jit(solution)/shard_map/all_gather | solution.py:75
  497.0 70.2 %copy-start.3 = (f32[2,144]{1,0:T(2,128)S(1)}, f32[2,144]{1,0:T(2,128)}, u32[]{:S(2)}) copy-start(f32[2,144]{1,0:T(2,128)} %param.14) | copy-start | bytes 3460
  497.0 70.2 %copy-start.4 = (bf16[2,144]{1,0:T(2,128)(2,1)S(1)}, bf16[2,144]{1,0:T(2,128)(2,1)}, u32[]{:S(2)}) copy-start(bf16[2,144]{1,0:T(2,128)(2,1)} %param.11) | copy-start | bytes 1732
Sparse Core Ops, SparseCore 0:
  19.9 40.8 reduce-scatter.2
  63.7 39.5 reduce-scatter.4
  155.1 145.2 all-reduce.2
  350.1 142.4 all-reduce.4
  497.1 36.2 all-gather.2
